TPU v7x, 512 devices: a whole 4x8x8 slice. The times are simulated.
512 devices in a mesh: ctx: 32 (over z, x_hi, core), head: 16 (over x_lo, y).
Axes of the slice: x: 4 (x_hi: 2, x_lo: 2; x = x_hi * 2 + x_lo), y: 8, z: 8, core: 2. Of those that a mesh axis runs over, the one named last changes fastest.
Arguments:
- queries: bfloat16 [8192, 8192], P(('ctx', 'head')), may hold values from -6 to 6
- keys: bfloat16 [8192, 1024], P('ctx'), may hold values from -6 to 6
- values: bfloat16 [8192, 1024], P('ctx'), may hold values from -6 to 6
- doc_lengths: int32 [16], replicated, may hold values from 1 to 2048, 8192 in all
- slot_source: int32 [512], replicated, may hold values from 0 to 511, as said below
Outputs:
- attended: bfloat16 [8192, 8192], P('ctx', 'head')
Inputs may be any that keep to these rules, and one draw needn't show every extreme that they name: `slot_source`: each piece appears in exactly one slot; a piece keeps its place within its block of 256 // 16 pieces (slot s holds a piece c with s and c equal modulo that count), and the pieces of one block of 256 // 16 go to as many different blocks of slots.
All inputs are finite; a program needn't handle non-finite values.
Results may differ from a plain program's by a relative error of at most 0.0036.
Values may be sent and summed in bfloat16 or wider, within the bound.
A program may use at most 128 MiB of HBM per device.

v0:
```python
import jax
import jax.numpy as jnp
from jax import lax
from jax.sharding import PartitionSpec as P

HD = 128
GROUP = 8


def passed_along(block, axis, distance):
    devices = range(lax.axis_size(axis))
    route = [((i - distance) % len(devices), i) for i in devices]
    return lax.ppermute(block, axis, route)


def local(queries, keys, values, doc_lengths, slot_source):
    ctx_count = lax.axis_size("ctx")
    ctx_index = lax.axis_index("ctx")
    head_index = lax.axis_index("head")
    local_q = lax.all_to_all(queries, "head", split_axis=1, concat_axis=0, tiled=True)
    rows = local_q.shape[0]
    width = local_q.shape[1]
    heads = width // HD
    piece_rows = 2 * rows // ctx_count
    count = rows // piece_rows
    total_pieces = slot_source.shape[0]
    order = jnp.arange(total_pieces, dtype=jnp.int32)
    match = slot_source[:, None] == order[None, :]
    slot_of = jnp.sum(jnp.where(match, order[:, None], 0), axis=0)
    target = lax.dynamic_slice_in_dim(slot_of, ctx_index * count, count) // count
    peers = jnp.arange(ctx_count, dtype=jnp.int32)
    select = (peers[:, None] == target[None, :]).astype(jnp.bfloat16)
    sources = lax.dynamic_slice_in_dim(slot_source, ctx_index * count, count)
    pick = (sources[:, None] // count == peers[None, :]).astype(jnp.bfloat16)

    def route(data):
        blocks = data.reshape(count, piece_rows, width)
        outgoing = jnp.einsum(
            "pk,kcf->pcf", select, blocks, preferred_element_type=jnp.float32
        ).astype(jnp.bfloat16)
        incoming = lax.all_to_all(outgoing, "ctx", split_axis=0, concat_axis=0, tiled=True)
        placed = jnp.einsum(
            "lp,pcf->lcf", pick, incoming, preferred_element_type=jnp.float32
        ).astype(jnp.bfloat16)
        return placed.reshape(rows, width)

    owned = route(local_q).reshape(rows, heads, HD)
    q_pos = (
        sources[:, None] * piece_rows + jnp.arange(piece_rows, dtype=jnp.int32)[None, :]
    ).reshape(rows)
    ends = jnp.cumsum(doc_lengths)
    q_doc = jnp.sum((ends[None, :] <= q_pos[:, None]).astype(jnp.int32), axis=-1)
    kv_head = head_index * heads // GROUP
    key_own = lax.dynamic_slice_in_dim(keys, kv_head * HD, HD, 1)
    value_own = lax.dynamic_slice_in_dim(values, kv_head * HD, HD, 1)
    paired = jnp.stack([key_own, value_own])
    scale = 1.0 / HD**0.5

    def absorb(state, allowed, block):
        top, total, accum = state
        score = (
            jnp.einsum("chd,kd->hck", owned, block[0], preferred_element_type=jnp.float32) * scale
        )
        score = jnp.where(allowed[None], score, -1e30)
        peak = jnp.maximum(top, jnp.max(score, axis=-1))
        weight = jnp.where(allowed[None], jnp.exp(score - peak[..., None]), 0.0)
        factor = jnp.exp(top - peak)
        total = total * factor + jnp.sum(weight, axis=-1)
        accum = accum * factor[..., None] + jnp.einsum(
            "hck,kd->hcd", weight.astype(jnp.bfloat16), block[1], preferred_element_type=jnp.float32
        )
        return (peak, total, accum)

    def update(state, block, k_start):
        k_pos = k_start + jnp.arange(block.shape[1], dtype=jnp.int32)
        k_doc = jnp.sum((ends[None, :] <= k_pos[:, None]).astype(jnp.int32), axis=-1)
        allowed = (k_doc[None, :] == q_doc[:, None]) & (k_pos[None, :] <= q_pos[:, None])
        return absorb(state, allowed, block)

    initial = (
        jnp.full((heads, rows), -1e30, jnp.float32),
        jnp.zeros((heads, rows), jnp.float32),
        jnp.zeros((heads, rows, HD), jnp.float32),
    )
    block_rows = paired.shape[1]
    state = update(initial, paired, ctx_index * block_rows)

    def next_block(step, carry):
        inner, current = carry
        current = passed_along(current, "ctx", 1)
        anchor = (ctx_index - step) % ctx_count
        return (update(inner, current, anchor * block_rows), current)

    state, last_block = lax.fori_loop(1, ctx_count, next_block, (state, paired))
    tops, totals, accums = state
    result = (accums / totals[..., None]).astype(jnp.bfloat16)
    result = jnp.transpose(result, (1, 0, 2)).reshape(rows, width)
    return result


def solution(mesh):
    return jax.shard_map(
        local,
        mesh=mesh,
        in_specs=(P(("ctx", "head"), None), P("ctx", None), P("ctx", None), P(), P()),
        out_specs=P("ctx", "head"),
        check_vma=False,
    )
```

profile of v0, /device:TPU:1, one launch (start us, length us, event | category | flops | bytes accessed | tf_op | source)
XLA Modules:
  0.0 392.6 jit_solution(3864306621019204526)
XLA Ops:
  1.7 8.7 %all-to-all-start = ((bf16[16,16,512]{2,0,1:T(8,128)(2,1)}), bf16[16,16,512]{2,0,1:T(8,128)(2,1)S(1)}, u32[]{:S(2)}, u32[]{:S(2)}) async-start(bf16[16,16,512]{2,0,1:T(8,128)(2,1)} %bitcast.50), calls=%async_computation | async-start | bytes 524288 | tf_op jit(solution)/shard_map/all_to_all | solution.py:20
  11.3 6.8 %all-to-all-done = bf16[16,16,512]{2,0,1:T(8,128)(2,1)S(1)} async-done(((bf16[16,16,512]{2,0,1:T(8,128)(2,1)}), bf16[16,16,512]{2,0,1:T(8,128)(2,1)S(1)}, u32[]{:S(2)}, u32[]{:S(2)}) %all-to-all-start) | async-done | bytes 262176 | tf_op jit(solution)/shard_map/all_to_all | solution.py:20
  19.6 15.9 %all-to-all-start.1 = ((bf16[32,16,512]{2,1,0:T(8,128)(2,1)}), bf16[32,16,512]{2,1,0:T(8,128)(2,1)S(1)}, u32[]{:S(2)}, u32[]{:S(2)}) async-start(bf16[32,16,512]{2,1,0:T(8,128)(2,1)} %copy.42), calls=%async_computation.1 | async-start | bytes 1048576 | tf_op jit(solution)/shard_map/all_to_all | solution.py:41
  37.9 14.7 %all-to-all-done.1 = bf16[32,16,512]{2,1,0:T(8,128)(2,1)S(1)} async-done(((bf16[32,16,512]{2,1,0:T(8,128)(2,1)}), bf16[32,16,512]{2,1,0:T(8,128)(2,1)S(1)}, u32[]{:S(2)}, u32[]{:S(2)}) %all-to-all-start.1) | async-done | bytes 524320 | tf_op jit(solution)/shard_map/all_to_all | solution.py:41
  56.0 335.7 %while.22 = (s32[]{:T(128)}, f32[4,256]{1,0:T(4,128)S(1)}, f32[4,256]{1,0:T(4,128)S(1)}, f32[4,256,128]{2,1,0:T(8,128)S(1)}, bf16[2,256,128]{2,1,0:T(8,128)(2,1)...) while((s32[]{:T(128)}, f32[4,256]{1,0:T(4,128)S(1)}, ...), condition=%wide.region_10.11_spmd.clone, body=%wide.region_6.10_spmd.clone.sunk | while | flops 137050384 | bytes 5712318 | solution.py:94
  56.0 5.7 %collective-permute-start = (bf16[2,256,128]{2,1,0:T(8,128)(2,1)S(1)}, bf16[2,256,128]{2,1,0:T(8,128)(2,1)S(1)}, u32[]{:S(2)}, u32[]{:S(2)}) collective-permute-start(bf16[2,256,128]{2,1,0:T(8,128)(2,1)S(1)} %get-tuple-element.436), channel_id=1, source_target_pairs={{496,0},{0,16},{16,32},{32,48},{48,64},{64,80},{80,96},{96,112},{1... | collective-permute-start | bytes 393224 | tf_op jit(solution)/shard_map/while/body/eval_jaxpr/ppermute | solution.py:13
  64.8 5.9 %collective-permute-start = (bf16[2,256,128]{2,1,0:T(8,128)(2,1)S(1)}, bf16[2,256,128]{2,1,0:T(8,128)(2,1)S(1)}, u32[]{:S(2)}, u32[]{:S(2)}) collective-permute-start(bf16[2,256,128]{2,1,0:T(8,128)(2,1)S(1)} %get-tuple-element.436), channel_id=1, source_target_pairs={{496,0},{0,16},{16,32},{32,48},{48,64},{64,80},{80,96},{96,112},{1... | collective-permute-start | bytes 393224 | tf_op jit(solution)/shard_map/while/body/eval_jaxpr/ppermute | solution.py:13
  73.7 5.9 %collective-permute-start = (bf16[2,256,128]{2,1,0:T(8,128)(2,1)S(1)}, bf16[2,256,128]{2,1,0:T(8,128)(2,1)S(1)}, u32[]{:S(2)}, u32[]{:S(2)}) collective-permute-start(bf16[2,256,128]{2,1,0:T(8,128)(2,1)S(1)} %get-tuple-element.436), channel_id=1, source_target_pairs={{496,0},{0,16},{16,32},{32,48},{48,64},{64,80},{80,96},{96,112},{1... | collective-permute-start | bytes 393224 | tf_op jit(solution)/shard_map/while/body/eval_jaxpr/ppermute | solution.py:13
  80.0 2.1 collective-permute-done
  83.2 5.3 %collective-permute-start = (bf16[2,256,128]{2,1,0:T(8,128)(2,1)S(1)}, bf16[2,256,128]{2,1,0:T(8,128)(2,1)S(1)}, u32[]{:S(2)}, u32[]{:S(2)}) collective-permute-start(bf16[2,256,128]{2,1,0:T(8,128)(2,1)S(1)} %get-tuple-element.436), channel_id=1, source_target_pairs={{496,0},{0,16},{16,32},{32,48},{48,64},{64,80},{80,96},{96,112},{1... | collective-permute-start | bytes 393224 | tf_op jit(solution)/shard_map/while/body/eval_jaxpr/ppermute | solution.py:13
  88.9 4.2 %collective-permute-done = bf16[2,256,128]{2,1,0:T(8,128)(2,1)S(1)} collective-permute-done((bf16[2,256,128]{2,1,0:T(8,128)(2,1)S(1)}, bf16[2,256,128]{2,1,0:T(8,128)(2,1)S(1)}, u32[]{:S(2)}, u32[]{:S(2)}) %collective-permute-start) | collective-permute-done | bytes 131104 | tf_op jit(solution)/shard_map/while/body/eval_jaxpr/ppermute | solution.py:13
  94.2 3.2 collective-permute-start
  97.8 6.3 %collective-permute-done = bf16[2,256,128]{2,1,0:T(8,128)(2,1)S(1)} collective-permute-done((bf16[2,256,128]{2,1,0:T(8,128)(2,1)S(1)}, bf16[2,256,128]{2,1,0:T(8,128)(2,1)S(1)}, u32[]{:S(2)}, u32[]{:S(2)}) %collective-permute-start) | collective-permute-done | bytes 131104 | tf_op jit(solution)/shard_map/while/body/eval_jaxpr/ppermute | solution.py:13
  105.2 1.9 collective-permute-start
  107.6 7.5 %collective-permute-done = bf16[2,256,128]{2,1,0:T(8,128)(2,1)S(1)} collective-permute-done((bf16[2,256,128]{2,1,0:T(8,128)(2,1)S(1)}, bf16[2,256,128]{2,1,0:T(8,128)(2,1)S(1)}, u32[]{:S(2)}, u32[]{:S(2)}) %collective-permute-start) | collective-permute-done | bytes 131104 | tf_op jit(solution)/shard_map/while/body/eval_jaxpr/ppermute | solution.py:13
  116.2 1.9 collective-permute-start
  118.6 7.5 %collective-permute-done = bf16[2,256,128]{2,1,0:T(8,128)(2,1)S(1)} collective-permute-done((bf16[2,256,128]{2,1,0:T(8,128)(2,1)S(1)}, bf16[2,256,128]{2,1,0:T(8,128)(2,1)S(1)}, u32[]{:S(2)}, u32[]{:S(2)}) %collective-permute-start) | collective-permute-done | bytes 131104 | tf_op jit(solution)/shard_map/while/body/eval_jaxpr/ppermute | solution.py:13
  127.3 1.9 collective-permute-start
  129.6 7.5 %collective-permute-done = bf16[2,256,128]{2,1,0:T(8,128)(2,1)S(1)} collective-permute-done((bf16[2,256,128]{2,1,0:T(8,128)(2,1)S(1)}, bf16[2,256,128]{2,1,0:T(8,128)(2,1)S(1)}, u32[]{:S(2)}, u32[]{:S(2)}) %collective-permute-start) | collective-permute-done | bytes 131104 | tf_op jit(solution)/shard_map/while/body/eval_jaxpr/ppermute | solution.py:13
  138.3 1.9 collective-permute-start
  140.6 7.5 %collective-permute-done = bf16[2,256,128]{2,1,0:T(8,128)(2,1)S(1)} collective-permute-done((bf16[2,256,128]{2,1,0:T(8,128)(2,1)S(1)}, bf16[2,256,128]{2,1,0:T(8,128)(2,1)S(1)}, u32[]{:S(2)}, u32[]{:S(2)}) %collective-permute-start) | collective-permute-done | bytes 131104 | tf_op jit(solution)/shard_map/while/body/eval_jaxpr/ppermute | solution.py:13
  149.3 1.9 collective-permute-start
  151.6 7.5 %collective-permute-done = bf16[2,256,128]{2,1,0:T(8,128)(2,1)S(1)} collective-permute-done((bf16[2,256,128]{2,1,0:T(8,128)(2,1)S(1)}, bf16[2,256,128]{2,1,0:T(8,128)(2,1)S(1)}, u32[]{:S(2)}, u32[]{:S(2)}) %collective-permute-start) | collective-permute-done | bytes 131104 | tf_op jit(solution)/shard_map/while/body/eval_jaxpr/ppermute | solution.py:13
  160.3 1.9 collective-permute-start
  162.7 7.5 %collective-permute-done = bf16[2,256,128]{2,1,0:T(8,128)(2,1)S(1)} collective-permute-done((bf16[2,256,128]{2,1,0:T(8,128)(2,1)S(1)}, bf16[2,256,128]{2,1,0:T(8,128)(2,1)S(1)}, u32[]{:S(2)}, u32[]{:S(2)}) %collective-permute-start) | collective-permute-done | bytes 131104 | tf_op jit(solution)/shard_map/while/body/eval_jaxpr/ppermute | solution.py:13
  171.3 1.9 collective-permute-start
  173.7 7.5 %collective-permute-done = bf16[2,256,128]{2,1,0:T(8,128)(2,1)S(1)} collective-permute-done((bf16[2,256,128]{2,1,0:T(8,128)(2,1)S(1)}, bf16[2,256,128]{2,1,0:T(8,128)(2,1)S(1)}, u32[]{:S(2)}, u32[]{:S(2)}) %collective-permute-start) | collective-permute-done | bytes 131104 | tf_op jit(solution)/shard_map/while/body/eval_jaxpr/ppermute | solution.py:13
  182.4 1.9 collective-permute-start
  184.7 7.5 %collective-permute-done = bf16[2,256,128]{2,1,0:T(8,128)(2,1)S(1)} collective-permute-done((bf16[2,256,128]{2,1,0:T(8,128)(2,1)S(1)}, bf16[2,256,128]{2,1,0:T(8,128)(2,1)S(1)}, u32[]{:S(2)}, u32[]{:S(2)}) %collective-permute-start) | collective-permute-done | bytes 131104 | tf_op jit(solution)/shard_map/while/body/eval_jaxpr/ppermute | solution.py:13
  193.4 1.9 collective-permute-start
  195.7 7.5 %collective-permute-done = bf16[2,256,128]{2,1,0:T(8,128)(2,1)S(1)} collective-permute-done((bf16[2,256,128]{2,1,0:T(8,128)(2,1)S(1)}, bf16[2,256,128]{2,1,0:T(8,128)(2,1)S(1)}, u32[]{:S(2)}, u32[]{:S(2)}) %collective-permute-start) | collective-permute-done | bytes 131104 | tf_op jit(solution)/shard_map/while/body/eval_jaxpr/ppermute | solution.py:13
  204.4 1.9 collective-permute-start
  206.7 7.5 %collective-permute-done = bf16[2,256,128]{2,1,0:T(8,128)(2,1)S(1)} collective-permute-done((bf16[2,256,128]{2,1,0:T(8,128)(2,1)S(1)}, bf16[2,256,128]{2,1,0:T(8,128)(2,1)S(1)}, u32[]{:S(2)}, u32[]{:S(2)}) %collective-permute-start) | collective-permute-done | bytes 131104 | tf_op jit(solution)/shard_map/while/body/eval_jaxpr/ppermute | solution.py:13
  215.4 1.9 collective-permute-start
  217.8 7.5 %collective-permute-done = bf16[2,256,128]{2,1,0:T(8,128)(2,1)S(1)} collective-permute-done((bf16[2,256,128]{2,1,0:T(8,128)(2,1)S(1)}, bf16[2,256,128]{2,1,0:T(8,128)(2,1)S(1)}, u32[]{:S(2)}, u32[]{:S(2)}) %collective-permute-start) | collective-permute-done | bytes 131104 | tf_op jit(solution)/shard_map/while/body/eval_jaxpr/ppermute | solution.py:13
  226.4 1.9 collective-permute-start
  228.8 7.5 %collective-permute-done = bf16[2,256,128]{2,1,0:T(8,128)(2,1)S(1)} collective-permute-done((bf16[2,256,128]{2,1,0:T(8,128)(2,1)S(1)}, bf16[2,256,128]{2,1,0:T(8,128)(2,1)S(1)}, u32[]{:S(2)}, u32[]{:S(2)}) %collective-permute-start) | collective-permute-done | bytes 131104 | tf_op jit(solution)/shard_map/while/body/eval_jaxpr/ppermute | solution.py:13
  237.4 1.9 collective-permute-start
  239.8 7.5 %collective-permute-done = bf16[2,256,128]{2,1,0:T(8,128)(2,1)S(1)} collective-permute-done((bf16[2,256,128]{2,1,0:T(8,128)(2,1)S(1)}, bf16[2,256,128]{2,1,0:T(8,128)(2,1)S(1)}, u32[]{:S(2)}, u32[]{:S(2)}) %collective-permute-start) | collective-permute-done | bytes 131104 | tf_op jit(solution)/shard_map/while/body/eval_jaxpr/ppermute | solution.py:13
  248.5 1.9 collective-permute-start
  250.8 7.5 %collective-permute-done = bf16[2,256,128]{2,1,0:T(8,128)(2,1)S(1)} collective-permute-done((bf16[2,256,128]{2,1,0:T(8,128)(2,1)S(1)}, bf16[2,256,128]{2,1,0:T(8,128)(2,1)S(1)}, u32[]{:S(2)}, u32[]{:S(2)}) %collective-permute-start) | collective-permute-done | bytes 131104 | tf_op jit(solution)/shard_map/while/body/eval_jaxpr/ppermute | solution.py:13
  259.5 1.9 collective-permute-start
  261.8 7.5 %collective-permute-done = bf16[2,256,128]{2,1,0:T(8,128)(2,1)S(1)} collective-permute-done((bf16[2,256,128]{2,1,0:T(8,128)(2,1)S(1)}, bf16[2,256,128]{2,1,0:T(8,128)(2,1)S(1)}, u32[]{:S(2)}, u32[]{:S(2)}) %collective-permute-start) | collective-permute-done | bytes 131104 | tf_op jit(solution)/shard_map/while/body/eval_jaxpr/ppermute | solution.py:13
  270.5 1.9 collective-permute-start
  272.9 7.5 %collective-permute-done = bf16[2,256,128]{2,1,0:T(8,128)(2,1)S(1)} collective-permute-done((bf16[2,256,128]{2,1,0:T(8,128)(2,1)S(1)}, bf16[2,256,128]{2,1,0:T(8,128)(2,1)S(1)}, u32[]{:S(2)}, u32[]{:S(2)}) %collective-permute-start) | collective-permute-done | bytes 131104 | tf_op jit(solution)/shard_map/while/body/eval_jaxpr/ppermute | solution.py:13
  281.5 1.9 collective-permute-start
  283.9 7.5 %collective-permute-done = bf16[2,256,128]{2,1,0:T(8,128)(2,1)S(1)} collective-permute-done((bf16[2,256,128]{2,1,0:T(8,128)(2,1)S(1)}, bf16[2,256,128]{2,1,0:T(8,128)(2,1)S(1)}, u32[]{:S(2)}, u32[]{:S(2)}) %collective-permute-start) | collective-permute-done | bytes 131104 | tf_op jit(solution)/shard_map/while/body/eval_jaxpr/ppermute | solution.py:13
  292.5 1.9 collective-permute-start
  294.9 7.5 %collective-permute-done = bf16[2,256,128]{2,1,0:T(8,128)(2,1)S(1)} collective-permute-done((bf16[2,256,128]{2,1,0:T(8,128)(2,1)S(1)}, bf16[2,256,128]{2,1,0:T(8,128)(2,1)S(1)}, u32[]{:S(2)}, u32[]{:S(2)}) %collective-permute-start) | collective-permute-done | bytes 131104 | tf_op jit(solution)/shard_map/while/body/eval_jaxpr/ppermute | solution.py:13
  303.6 1.9 collective-permute-start
  305.9 7.5 %collective-permute-done = bf16[2,256,128]{2,1,0:T(8,128)(2,1)S(1)} collective-permute-done((bf16[2,256,128]{2,1,0:T(8,128)(2,1)S(1)}, bf16[2,256,128]{2,1,0:T(8,128)(2,1)S(1)}, u32[]{:S(2)}, u32[]{:S(2)}) %collective-permute-start) | collective-permute-done | bytes 131104 | tf_op jit(solution)/shard_map/while/body/eval_jaxpr/ppermute | solution.py:13
  314.6 1.9 collective-permute-start
  316.9 7.5 %collective-permute-done = bf16[2,256,128]{2,1,0:T(8,128)(2,1)S(1)} collective-permute-done((bf16[2,256,128]{2,1,0:T(8,128)(2,1)S(1)}, bf16[2,256,128]{2,1,0:T(8,128)(2,1)S(1)}, u32[]{:S(2)}, u32[]{:S(2)}) %collective-permute-start) | collective-permute-done | bytes 131104 | tf_op jit(solution)/shard_map/while/body/eval_jaxpr/ppermute | solution.py:13
  325.6 1.9 collective-permute-start
  328.0 7.5 %collective-permute-done = bf16[2,256,128]{2,1,0:T(8,128)(2,1)S(1)} collective-permute-done((bf16[2,256,128]{2,1,0:T(8,128)(2,1)S(1)}, bf16[2,256,128]{2,1,0:T(8,128)(2,1)S(1)}, u32[]{:S(2)}, u32[]{:S(2)}) %collective-permute-start) | collective-permute-done | bytes 131104 | tf_op jit(solution)/shard_map/while/body/eval_jaxpr/ppermute | solution.py:13
  336.6 1.9 collective-permute-start
  339.0 7.5 %collective-permute-done = bf16[2,256,128]{2,1,0:T(8,128)(2,1)S(1)} collective-permute-done((bf16[2,256,128]{2,1,0:T(8,128)(2,1)S(1)}, bf16[2,256,128]{2,1,0:T(8,128)(2,1)S(1)}, u32[]{:S(2)}, u32[]{:S(2)}) %collective-permute-start) | collective-permute-done | bytes 131104 | tf_op jit(solution)/shard_map/while/body/eval_jaxpr/ppermute | solution.py:13
  347.6 1.9 collective-permute-start
  350.0 7.5 %collective-permute-done = bf16[2,256,128]{2,1,0:T(8,128)(2,1)S(1)} collective-permute-done((bf16[2,256,128]{2,1,0:T(8,128)(2,1)S(1)}, bf16[2,256,128]{2,1,0:T(8,128)(2,1)S(1)}, u32[]{:S(2)}, u32[]{:S(2)}) %collective-permute-start) | collective-permute-done | bytes 131104 | tf_op jit(solution)/shard_map/while/body/eval_jaxpr/ppermute | solution.py:13
  358.7 1.9 collective-permute-start
  361.0 7.5 %collective-permute-done = bf16[2,256,128]{2,1,0:T(8,128)(2,1)S(1)} collective-permute-done((bf16[2,256,128]{2,1,0:T(8,128)(2,1)S(1)}, bf16[2,256,128]{2,1,0:T(8,128)(2,1)S(1)}, u32[]{:S(2)}, u32[]{:S(2)}) %collective-permute-start) | collective-permute-done | bytes 131104 | tf_op jit(solution)/shard_map/while/body/eval_jaxpr/ppermute | solution.py:13
  372.0 7.5 %collective-permute-done = bf16[2,256,128]{2,1,0:T(8,128)(2,1)S(1)} collective-permute-done((bf16[2,256,128]{2,1,0:T(8,128)(2,1)S(1)}, bf16[2,256,128]{2,1,0:T(8,128)(2,1)S(1)}, u32[]{:S(2)}, u32[]{:S(2)}) %collective-permute-start) | collective-permute-done | bytes 131104 | tf_op jit(solution)/shard_map/while/body/eval_jaxpr/ppermute | solution.py:13
  380.7 1.9 collective-permute-start
  383.0 7.5 %collective-permute-done = bf16[2,256,128]{2,1,0:T(8,128)(2,1)S(1)} collective-permute-done((bf16[2,256,128]{2,1,0:T(8,128)(2,1)S(1)}, bf16[2,256,128]{2,1,0:T(8,128)(2,1)S(1)}, u32[]{:S(2)}, u32[]{:S(2)}) %collective-permute-start) | collective-permute-done | bytes 131104 | tf_op jit(solution)/shard_map/while/body/eval_jaxpr/ppermute | solution.py:13
  (405 shorter events, 60.8 us)
Async XLA Ops:
  1.7 16.5 %all-to-all-start = ((bf16[16,16,512]{2,0,1:T(8,128)(2,1)}), bf16[16,16,512]{2,0,1:T(8,128)(2,1)S(1)}, u32[]{:S(2)}, u32[]{:S(2)}) async-start(bf16[16,16,512]{2,0,1:T(8,128)(2,1)} %bitcast.50), calls=%async_computation | async-start | bytes 524288 | tf_op jit(solution)/shard_map/all_to_all | solution.py:20
  10.4 0.7 copy-start
  19.6 33.0 %all-to-all-start.1 = ((bf16[32,16,512]{2,1,0:T(8,128)(2,1)}), bf16[32,16,512]{2,1,0:T(8,128)(2,1)S(1)}, u32[]{:S(2)}, u32[]{:S(2)}) async-start(bf16[32,16,512]{2,1,0:T(8,128)(2,1)} %copy.42), calls=%async_computation.1 | async-start | bytes 1048576 | tf_op jit(solution)/shard_map/all_to_all | solution.py:41
  35.8 0.7 copy-start.1
  56.0 7.7 %collective-permute-start = (bf16[2,256,128]{2,1,0:T(8,128)(2,1)S(1)}, bf16[2,256,128]{2,1,0:T(8,128)(2,1)S(1)}, u32[]{:S(2)}, u32[]{:S(2)}) collective-permute-start(bf16[2,256,128]{2,1,0:T(8,128)(2,1)S(1)} %get-tuple-element.436), channel_id=1, source_target_pairs={{496,0},{0,16},{16,32},{32,48},{48,64},{64,80},{80,96},{96,112},{1... | collective-permute-start | bytes 393224 | tf_op jit(solution)/shard_map/while/body/eval_jaxpr/ppermute | solution.py:13
  64.8 7.8 %collective-permute-start = (bf16[2,256,128]{2,1,0:T(8,128)(2,1)S(1)}, bf16[2,256,128]{2,1,0:T(8,128)(2,1)S(1)}, u32[]{:S(2)}, u32[]{:S(2)}) collective-permute-start(bf16[2,256,128]{2,1,0:T(8,128)(2,1)S(1)} %get-tuple-element.436), channel_id=1, source_target_pairs={{496,0},{0,16},{16,32},{32,48},{48,64},{64,80},{80,96},{96,112},{1... | collective-permute-start | bytes 393224 | tf_op jit(solution)/shard_map/while/body/eval_jaxpr/ppermute | solution.py:13
  73.7 8.3 %collective-permute-start = (bf16[2,256,128]{2,1,0:T(8,128)(2,1)S(1)}, bf16[2,256,128]{2,1,0:T(8,128)(2,1)S(1)}, u32[]{:S(2)}, u32[]{:S(2)}) collective-permute-start(bf16[2,256,128]{2,1,0:T(8,128)(2,1)S(1)} %get-tuple-element.436), channel_id=1, source_target_pairs={{496,0},{0,16},{16,32},{32,48},{48,64},{64,80},{80,96},{96,112},{1... | collective-permute-start | bytes 393224 | tf_op jit(solution)/shard_map/while/body/eval_jaxpr/ppermute | solution.py:13
  83.2 9.9 %collective-permute-start = (bf16[2,256,128]{2,1,0:T(8,128)(2,1)S(1)}, bf16[2,256,128]{2,1,0:T(8,128)(2,1)S(1)}, u32[]{:S(2)}, u32[]{:S(2)}) collective-permute-start(bf16[2,256,128]{2,1,0:T(8,128)(2,1)S(1)} %get-tuple-element.436), channel_id=1, source_target_pairs={{496,0},{0,16},{16,32},{32,48},{48,64},{64,80},{80,96},{96,112},{1... | collective-permute-start | bytes 393224 | tf_op jit(solution)/shard_map/while/body/eval_jaxpr/ppermute | solution.py:13
  94.2 9.9 %collective-permute-start = (bf16[2,256,128]{2,1,0:T(8,128)(2,1)S(1)}, bf16[2,256,128]{2,1,0:T(8,128)(2,1)S(1)}, u32[]{:S(2)}, u32[]{:S(2)}) collective-permute-start(bf16[2,256,128]{2,1,0:T(8,128)(2,1)S(1)} %get-tuple-element.436), channel_id=1, source_target_pairs={{496,0},{0,16},{16,32},{32,48},{48,64},{64,80},{80,96},{96,112},{1... | collective-permute-start | bytes 393224 | tf_op jit(solution)/shard_map/while/body/eval_jaxpr/ppermute | solution.py:13
  105.2 9.9 %collective-permute-start = (bf16[2,256,128]{2,1,0:T(8,128)(2,1)S(1)}, bf16[2,256,128]{2,1,0:T(8,128)(2,1)S(1)}, u32[]{:S(2)}, u32[]{:S(2)}) collective-permute-start(bf16[2,256,128]{2,1,0:T(8,128)(2,1)S(1)} %get-tuple-element.436), channel_id=1, source_target_pairs={{496,0},{0,16},{16,32},{32,48},{48,64},{64,80},{80,96},{96,112},{1... | collective-permute-start | bytes 393224 | tf_op jit(solution)/shard_map/while/body/eval_jaxpr/ppermute | solution.py:13
  116.2 9.9 %collective-permute-start = (bf16[2,256,128]{2,1,0:T(8,128)(2,1)S(1)}, bf16[2,256,128]{2,1,0:T(8,128)(2,1)S(1)}, u32[]{:S(2)}, u32[]{:S(2)}) collective-permute-start(bf16[2,256,128]{2,1,0:T(8,128)(2,1)S(1)} %get-tuple-element.436), channel_id=1, source_target_pairs={{496,0},{0,16},{16,32},{32,48},{48,64},{64,80},{80,96},{96,112},{1... | collective-permute-start | bytes 393224 | tf_op jit(solution)/shard_map/while/body/eval_jaxpr/ppermute | solution.py:13
  127.3 9.9 %collective-permute-start = (bf16[2,256,128]{2,1,0:T(8,128)(2,1)S(1)}, bf16[2,256,128]{2,1,0:T(8,128)(2,1)S(1)}, u32[]{:S(2)}, u32[]{:S(2)}) collective-permute-start(bf16[2,256,128]{2,1,0:T(8,128)(2,1)S(1)} %get-tuple-element.436), channel_id=1, source_target_pairs={{496,0},{0,16},{16,32},{32,48},{48,64},{64,80},{80,96},{96,112},{1... | collective-permute-start | bytes 393224 | tf_op jit(solution)/shard_map/while/body/eval_jaxpr/ppermute | solution.py:13
  138.3 9.9 %collective-permute-start = (bf16[2,256,128]{2,1,0:T(8,128)(2,1)S(1)}, bf16[2,256,128]{2,1,0:T(8,128)(2,1)S(1)}, u32[]{:S(2)}, u32[]{:S(2)}) collective-permute-start(bf16[2,256,128]{2,1,0:T(8,128)(2,1)S(1)} %get-tuple-element.436), channel_id=1, source_target_pairs={{496,0},{0,16},{16,32},{32,48},{48,64},{64,80},{80,96},{96,112},{1... | collective-permute-start | bytes 393224 | tf_op jit(solution)/shard_map/while/body/eval_jaxpr/ppermute | solution.py:13
  149.3 9.9 %collective-permute-start = (bf16[2,256,128]{2,1,0:T(8,128)(2,1)S(1)}, bf16[2,256,128]{2,1,0:T(8,128)(2,1)S(1)}, u32[]{:S(2)}, u32[]{:S(2)}) collective-permute-start(bf16[2,256,128]{2,1,0:T(8,128)(2,1)S(1)} %get-tuple-element.436), channel_id=1, source_target_pairs={{496,0},{0,16},{16,32},{32,48},{48,64},{64,80},{80,96},{96,112},{1... | collective-permute-start | bytes 393224 | tf_op jit(solution)/shard_map/while/body/eval_jaxpr/ppermute | solution.py:13
  160.3 9.9 %collective-permute-start = (bf16[2,256,128]{2,1,0:T(8,128)(2,1)S(1)}, bf16[2,256,128]{2,1,0:T(8,128)(2,1)S(1)}, u32[]{:S(2)}, u32[]{:S(2)}) collective-permute-start(bf16[2,256,128]{2,1,0:T(8,128)(2,1)S(1)} %get-tuple-element.436), channel_id=1, source_target_pairs={{496,0},{0,16},{16,32},{32,48},{48,64},{64,80},{80,96},{96,112},{1... | collective-permute-start | bytes 393224 | tf_op jit(solution)/shard_map/while/body/eval_jaxpr/ppermute | solution.py:13
  171.3 9.9 %collective-permute-start = (bf16[2,256,128]{2,1,0:T(8,128)(2,1)S(1)}, bf16[2,256,128]{2,1,0:T(8,128)(2,1)S(1)}, u32[]{:S(2)}, u32[]{:S(2)}) collective-permute-start(bf16[2,256,128]{2,1,0:T(8,128)(2,1)S(1)} %get-tuple-element.436), channel_id=1, source_target_pairs={{496,0},{0,16},{16,32},{32,48},{48,64},{64,80},{80,96},{96,112},{1... | collective-permute-start | bytes 393224 | tf_op jit(solution)/shard_map/while/body/eval_jaxpr/ppermute | solution.py:13
  182.4 9.9 %collective-permute-start = (bf16[2,256,128]{2,1,0:T(8,128)(2,1)S(1)}, bf16[2,256,128]{2,1,0:T(8,128)(2,1)S(1)}, u32[]{:S(2)}, u32[]{:S(2)}) collective-permute-start(bf16[2,256,128]{2,1,0:T(8,128)(2,1)S(1)} %get-tuple-element.436), channel_id=1, source_target_pairs={{496,0},{0,16},{16,32},{32,48},{48,64},{64,80},{80,96},{96,112},{1... | collective-permute-start | bytes 393224 | tf_op jit(solution)/shard_map/while/body/eval_jaxpr/ppermute | solution.py:13
  193.4 9.9 %collective-permute-start = (bf16[2,256,128]{2,1,0:T(8,128)(2,1)S(1)}, bf16[2,256,128]{2,1,0:T(8,128)(2,1)S(1)}, u32[]{:S(2)}, u32[]{:S(2)}) collective-permute-start(bf16[2,256,128]{2,1,0:T(8,128)(2,1)S(1)} %get-tuple-element.436), channel_id=1, source_target_pairs={{496,0},{0,16},{16,32},{32,48},{48,64},{64,80},{80,96},{96,112},{1... | collective-permute-start | bytes 393224 | tf_op jit(solution)/shard_map/while/body/eval_jaxpr/ppermute | solution.py:13
  204.4 9.9 %collective-permute-start = (bf16[2,256,128]{2,1,0:T(8,128)(2,1)S(1)}, bf16[2,256,128]{2,1,0:T(8,128)(2,1)S(1)}, u32[]{:S(2)}, u32[]{:S(2)}) collective-permute-start(bf16[2,256,128]{2,1,0:T(8,128)(2,1)S(1)} %get-tuple-element.436), channel_id=1, source_target_pairs={{496,0},{0,16},{16,32},{32,48},{48,64},{64,80},{80,96},{96,112},{1... | collective-permute-start | bytes 393224 | tf_op jit(solution)/shard_map/while/body/eval_jaxpr/ppermute | solution.py:13
  215.4 9.9 %collective-permute-start = (bf16[2,256,128]{2,1,0:T(8,128)(2,1)S(1)}, bf16[2,256,128]{2,1,0:T(8,128)(2,1)S(1)}, u32[]{:S(2)}, u32[]{:S(2)}) collective-permute-start(bf16[2,256,128]{2,1,0:T(8,128)(2,1)S(1)} %get-tuple-element.436), channel_id=1, source_target_pairs={{496,0},{0,16},{16,32},{32,48},{48,64},{64,80},{80,96},{96,112},{1... | collective-permute-start | bytes 393224 | tf_op jit(solution)/shard_map/while/body/eval_jaxpr/ppermute | solution.py:13
  226.4 9.9 %collective-permute-start = (bf16[2,256,128]{2,1,0:T(8,128)(2,1)S(1)}, bf16[2,256,128]{2,1,0:T(8,128)(2,1)S(1)}, u32[]{:S(2)}, u32[]{:S(2)}) collective-permute-start(bf16[2,256,128]{2,1,0:T(8,128)(2,1)S(1)} %get-tuple-element.436), channel_id=1, source_target_pairs={{496,0},{0,16},{16,32},{32,48},{48,64},{64,80},{80,96},{96,112},{1... | collective-permute-start | bytes 393224 | tf_op jit(solution)/shard_map/while/body/eval_jaxpr/ppermute | solution.py:13
  237.4 9.9 %collective-permute-start = (bf16[2,256,128]{2,1,0:T(8,128)(2,1)S(1)}, bf16[2,256,128]{2,1,0:T(8,128)(2,1)S(1)}, u32[]{:S(2)}, u32[]{:S(2)}) collective-permute-start(bf16[2,256,128]{2,1,0:T(8,128)(2,1)S(1)} %get-tuple-element.436), channel_id=1, source_target_pairs={{496,0},{0,16},{16,32},{32,48},{48,64},{64,80},{80,96},{96,112},{1... | collective-permute-start | bytes 393224 | tf_op jit(solution)/shard_map/while/body/eval_jaxpr/ppermute | solution.py:13
  248.5 9.9 %collective-permute-start = (bf16[2,256,128]{2,1,0:T(8,128)(2,1)S(1)}, bf16[2,256,128]{2,1,0:T(8,128)(2,1)S(1)}, u32[]{:S(2)}, u32[]{:S(2)}) collective-permute-start(bf16[2,256,128]{2,1,0:T(8,128)(2,1)S(1)} %get-tuple-element.436), channel_id=1, source_target_pairs={{496,0},{0,16},{16,32},{32,48},{48,64},{64,80},{80,96},{96,112},{1... | collective-permute-start | bytes 393224 | tf_op jit(solution)/shard_map/while/body/eval_jaxpr/ppermute | solution.py:13
  259.5 9.9 %collective-permute-start = (bf16[2,256,128]{2,1,0:T(8,128)(2,1)S(1)}, bf16[2,256,128]{2,1,0:T(8,128)(2,1)S(1)}, u32[]{:S(2)}, u32[]{:S(2)}) collective-permute-start(bf16[2,256,128]{2,1,0:T(8,128)(2,1)S(1)} %get-tuple-element.436), channel_id=1, source_target_pairs={{496,0},{0,16},{16,32},{32,48},{48,64},{64,80},{80,96},{96,112},{1... | collective-permute-start | bytes 393224 | tf_op jit(solution)/shard_map/while/body/eval_jaxpr/ppermute | solution.py:13
  270.5 9.9 %collective-permute-start = (bf16[2,256,128]{2,1,0:T(8,128)(2,1)S(1)}, bf16[2,256,128]{2,1,0:T(8,128)(2,1)S(1)}, u32[]{:S(2)}, u32[]{:S(2)}) collective-permute-start(bf16[2,256,128]{2,1,0:T(8,128)(2,1)S(1)} %get-tuple-element.436), channel_id=1, source_target_pairs={{496,0},{0,16},{16,32},{32,48},{48,64},{64,80},{80,96},{96,112},{1... | collective-permute-start | bytes 393224 | tf_op jit(solution)/shard_map/while/body/eval_jaxpr/ppermute | solution.py:13
  281.5 9.9 %collective-permute-start = (bf16[2,256,128]{2,1,0:T(8,128)(2,1)S(1)}, bf16[2,256,128]{2,1,0:T(8,128)(2,1)S(1)}, u32[]{:S(2)}, u32[]{:S(2)}) collective-permute-start(bf16[2,256,128]{2,1,0:T(8,128)(2,1)S(1)} %get-tuple-element.436), channel_id=1, source_target_pairs={{496,0},{0,16},{16,32},{32,48},{48,64},{64,80},{80,96},{96,112},{1... | collective-permute-start | bytes 393224 | tf_op jit(solution)/shard_map/while/body/eval_jaxpr/ppermute | solution.py:13
  292.5 9.9 %collective-permute-start = (bf16[2,256,128]{2,1,0:T(8,128)(2,1)S(1)}, bf16[2,256,128]{2,1,0:T(8,128)(2,1)S(1)}, u32[]{:S(2)}, u32[]{:S(2)}) collective-permute-start(bf16[2,256,128]{2,1,0:T(8,128)(2,1)S(1)} %get-tuple-element.436), channel_id=1, source_target_pairs={{496,0},{0,16},{16,32},{32,48},{48,64},{64,80},{80,96},{96,112},{1... | collective-permute-start | bytes 393224 | tf_op jit(solution)/shard_map/while/body/eval_jaxpr/ppermute | solution.py:13
  303.6 9.9 %collective-permute-start = (bf16[2,256,128]{2,1,0:T(8,128)(2,1)S(1)}, bf16[2,256,128]{2,1,0:T(8,128)(2,1)S(1)}, u32[]{:S(2)}, u32[]{:S(2)}) collective-permute-start(bf16[2,256,128]{2,1,0:T(8,128)(2,1)S(1)} %get-tuple-element.436), channel_id=1, source_target_pairs={{496,0},{0,16},{16,32},{32,48},{48,64},{64,80},{80,96},{96,112},{1... | collective-permute-start | bytes 393224 | tf_op jit(solution)/shard_map/while/body/eval_jaxpr/ppermute | solution.py:13
  314.6 9.9 %collective-permute-start = (bf16[2,256,128]{2,1,0:T(8,128)(2,1)S(1)}, bf16[2,256,128]{2,1,0:T(8,128)(2,1)S(1)}, u32[]{:S(2)}, u32[]{:S(2)}) collective-permute-start(bf16[2,256,128]{2,1,0:T(8,128)(2,1)S(1)} %get-tuple-element.436), channel_id=1, source_target_pairs={{496,0},{0,16},{16,32},{32,48},{48,64},{64,80},{80,96},{96,112},{1... | collective-permute-start | bytes 393224 | tf_op jit(solution)/shard_map/while/body/eval_jaxpr/ppermute | solution.py:13
  325.6 9.9 %collective-permute-start = (bf16[2,256,128]{2,1,0:T(8,128)(2,1)S(1)}, bf16[2,256,128]{2,1,0:T(8,128)(2,1)S(1)}, u32[]{:S(2)}, u32[]{:S(2)}) collective-permute-start(bf16[2,256,128]{2,1,0:T(8,128)(2,1)S(1)} %get-tuple-element.436), channel_id=1, source_target_pairs={{496,0},{0,16},{16,32},{32,48},{48,64},{64,80},{80,96},{96,112},{1... | collective-permute-start | bytes 393224 | tf_op jit(solution)/shard_map/while/body/eval_jaxpr/ppermute | solution.py:13
  336.6 9.9 %collective-permute-start = (bf16[2,256,128]{2,1,0:T(8,128)(2,1)S(1)}, bf16[2,256,128]{2,1,0:T(8,128)(2,1)S(1)}, u32[]{:S(2)}, u32[]{:S(2)}) collective-permute-start(bf16[2,256,128]{2,1,0:T(8,128)(2,1)S(1)} %get-tuple-element.436), channel_id=1, source_target_pairs={{496,0},{0,16},{16,32},{32,48},{48,64},{64,80},{80,96},{96,112},{1... | collective-permute-start | bytes 393224 | tf_op jit(solution)/shard_map/while/body/eval_jaxpr/ppermute | solution.py:13
  347.6 9.9 %collective-permute-start = (bf16[2,256,128]{2,1,0:T(8,128)(2,1)S(1)}, bf16[2,256,128]{2,1,0:T(8,128)(2,1)S(1)}, u32[]{:S(2)}, u32[]{:S(2)}) collective-permute-start(bf16[2,256,128]{2,1,0:T(8,128)(2,1)S(1)} %get-tuple-element.436), channel_id=1, source_target_pairs={{496,0},{0,16},{16,32},{32,48},{48,64},{64,80},{80,96},{96,112},{1... | collective-permute-start | bytes 393224 | tf_op jit(solution)/shard_map/while/body/eval_jaxpr/ppermute | solution.py:13
  358.7 9.9 %collective-permute-start = (bf16[2,256,128]{2,1,0:T(8,128)(2,1)S(1)}, bf16[2,256,128]{2,1,0:T(8,128)(2,1)S(1)}, u32[]{:S(2)}, u32[]{:S(2)}) collective-permute-start(bf16[2,256,128]{2,1,0:T(8,128)(2,1)S(1)} %get-tuple-element.436), channel_id=1, source_target_pairs={{496,0},{0,16},{16,32},{32,48},{48,64},{64,80},{80,96},{96,112},{1... | collective-permute-start | bytes 393224 | tf_op jit(solution)/shard_map/while/body/eval_jaxpr/ppermute | solution.py:13
  369.7 9.9 %collective-permute-start = (bf16[2,256,128]{2,1,0:T(8,128)(2,1)S(1)}, bf16[2,256,128]{2,1,0:T(8,128)(2,1)S(1)}, u32[]{:S(2)}, u32[]{:S(2)}) collective-permute-start(bf16[2,256,128]{2,1,0:T(8,128)(2,1)S(1)} %get-tuple-element.436), channel_id=1, source_target_pairs={{496,0},{0,16},{16,32},{32,48},{48,64},{64,80},{80,96},{96,112},{1... | collective-permute-start | bytes 393224 | tf_op jit(solution)/shard_map/while/body/eval_jaxpr/ppermute | solution.py:13
  380.7 9.9 %collective-permute-start = (bf16[2,256,128]{2,1,0:T(8,128)(2,1)S(1)}, bf16[2,256,128]{2,1,0:T(8,128)(2,1)S(1)}, u32[]{:S(2)}, u32[]{:S(2)}) collective-permute-start(bf16[2,256,128]{2,1,0:T(8,128)(2,1)S(1)} %get-tuple-element.436), channel_id=1, source_target_pairs={{496,0},{0,16},{16,32},{32,48},{48,64},{64,80},{80,96},{96,112},{1... | collective-permute-start | bytes 393224 | tf_op jit(solution)/shard_map/while/body/eval_jaxpr/ppermute | solution.py:13
where the time goes:
time: 400 us; the launch traced here: 393 us
  waiting for transfers between devices  233 us (58%)
  starting transfers between devices  101 us (25%)
  matrix products  28.9 us (7%)
  other arithmetic  18.5 us (5%)
  local copies, waits for them, and re-layouts  8.35 us (2%)
    ppermute x31, waiting for transfers between devices, passed_along(): return lax.ppermute(block, axis, route)  212 us
    ppermute x31, starting transfers between devices, passed_along(): return lax.ppermute(block, axis, route)  75.9 us
    dot_general x32, matrix products, absorb(): jnp.einsum('hck,kd->hcd', weight.astype(jnp.bfloat16), block[1], preferre...  16.9 us
    all_to_all x1, starting transfers between devices, route(): lax.all_to_all(outgoing, 'ctx', split_axis=0, concat_axis=0, tiled=True)  15.9 us
    all_to_all x1, waiting for transfers between devices, route(): lax.all_to_all(outgoing, 'ctx', split_axis=0, concat_axis=0, tiled=True)  14.7 us
    dot_general x32, matrix products, absorb(): jnp.einsum('chd,kd->hck', owned, block[0], preferred_element_type=jnp.flo...  11.2 us
    all_to_all x1, starting transfers between devices, local(): lax.all_to_all(queries, 'head', split_axis=1, concat_axis=0, tiled=True)  8.68 us
  transfers between devices with their start and end apart: 33, of which 33 were waited for; matrix products, arithmetic and copies ran while one was open for 4% of the time, Pallas kernels for 0%

commit v1 on v0

v1 whole, which is shorter than its diff:
```python
import functools
import math

import jax
import jax.numpy as jnp
from jax import lax
from jax.experimental import pallas as pl
from jax.experimental.pallas import tpu as pltpu
from jax.sharding import PartitionSpec as P

HD = 128
GROUP = 8
DOC_MAX = 2048
MASKED = -1e30
MESH = pl.DeviceIdType.MESH


def kernel(
    nctx, nhead, win, chunk,
    pick, slots, lengths, q_ref, k_ref, v_ref, o_ref,
    qbuf, kwin, vwin, bias, obuf, sbuf, rbuf,
    own_sem, q_send, q_recv, kv_send, kv_recv, f_send, f_recv, o_send, o_recv,
):
    ctx = lax.axis_index("ctx")
    head = lax.axis_index("head")
    piece, width = q_ref.shape[0], q_ref.shape[1] // nhead
    rows = k_ref.shape[0]
    count = rows // piece
    heads = width // HD
    chips = nctx // 2
    reach = win // 2
    core = lax.rem(ctx, 2)
    chip = ctx // 2
    sibling = chip * 2 + 1 - core

    barrier = pltpu.get_barrier_semaphore()

    @pl.loop(1, nctx)
    def _(t):
        pl.semaphore_signal(barrier, device_id=(lax.rem(ctx + t, nctx), head), device_id_type=MESH)

    @pl.loop(1, nhead)
    def _(t):
        pl.semaphore_signal(barrier, device_id=(ctx, lax.rem(head + t, nhead)), device_id_type=MESH)

    pl.semaphore_wait(barrier, nctx + nhead - 2)

    kv_cols = pl.ds(pl.multiple_of(((head * heads) // GROUP) * HD, HD), HD)

    def block(index):
        return pl.ds(pl.multiple_of(index * rows, rows), rows)

    def kv_copy(which, step):
        src = (k_ref, v_ref)[which]
        dst = (kwin, vwin)[which]
        return pltpu.make_async_remote_copy(
            src_ref=src.at[:, kv_cols],
            dst_ref=dst.at[block((reach - step) * 2 + core)],
            send_sem=kv_send.at[which, step],
            recv_sem=kv_recv.at[which, step],
            device_id=(lax.rem(chip + step, chips) * 2 + core, head),
            device_id_type=MESH,
        )

    def pass_copy(which, step):
        dst = (kwin, vwin)[which]
        spot = dst.at[block((reach - step) * 2 + core)]
        return pltpu.make_async_remote_copy(
            src_ref=spot,
            dst_ref=spot,
            send_sem=f_send.at[which, step],
            recv_sem=f_recv.at[which, step],
            device_id=(sibling, head),
            device_id_type=MESH,
        )

    def own_copy(which):
        src = (k_ref, v_ref)[which]
        dst = (kwin, vwin)[which]
        return pltpu.make_async_copy(src.at[:, kv_cols], dst.at[block(reach * 2 + core)], own_sem.at[which])

    for step in range(1, reach + 1):
        for which in range(2):
            kv_copy(which, step).start()
    for which in range(2):
        own_copy(which).start()

    def q_copy(t):
        peer = lax.rem(head + t, nhead)
        return pltpu.make_async_remote_copy(
            src_ref=q_ref.at[:, pl.ds(pl.multiple_of(peer * width, width), width)],
            dst_ref=qbuf.at[head],
            send_sem=q_send.at[t],
            recv_sem=q_recv.at[t],
            device_id=(ctx, peer),
            device_id_type=MESH,
        )

    @pl.loop(1, nhead)
    def _(t):
        q_copy(t).start()

    q_own = pltpu.make_async_copy(
        q_ref.at[:, pl.ds(pl.multiple_of(head * width, width), width)], qbuf.at[head], own_sem.at[2]
    )
    q_own.start()

    keys = (win + 1) * rows
    for lower in range(0, rows, chunk):
        line = lower + lax.broadcasted_iota(jnp.int32, (chunk, 1), 0)
        position = ctx * rows + line
        start = jnp.zeros((chunk, 1), jnp.int32)
        end = jnp.int32(0)
        for j in range(lengths.shape[0]):
            end = end + lengths[j]
            start = jnp.where(position >= end, end, start)
        start = start - (ctx - win) * rows
        for col in range(0, keys, rows):
            at = col + lax.broadcasted_iota(jnp.int32, (chunk, rows), 1)
            allowed = (at >= start) & (at <= win * rows + line)
            bias[lower : lower + chunk, col : col + rows] = jnp.where(allowed, 0.0, MASKED)

    for which in range(2):
        own_copy(which).wait()
        pass_copy(which, 0).start()
    for step in range(1, reach + 1):
        for which in range(2):
            kv_copy(which, step).wait_recv()
            pass_copy(which, step).start()
    q_own.wait()

    @pl.loop(1, nhead)
    def _(t):
        q_copy(t).wait_recv()

    for step in range(reach + 1):
        for which in range(2):
            pass_copy(which, step).wait_recv()

    seen = pl.ds(pl.multiple_of(core * rows, rows), keys)
    factor = math.log2(math.e) / HD**0.5

    def o_copy(h, t):
        owner = lax.rem(ctx + t, nctx)
        return pltpu.make_async_remote_copy(
            src_ref=sbuf.at[h, owner],
            dst_ref=rbuf.at[h, ctx],
            send_sem=o_send.at[h],
            recv_sem=o_recv.at[h],
            device_id=(owner, head),
            device_id_type=MESH,
        )

    @pl.loop(0, heads)
    def _(h):
        cols = pl.ds(pl.multiple_of(h * HD, HD), HD)
        for lower in range(0, rows, chunk):
            pieces = pl.ds(lower // piece, chunk // piece)
            query = qbuf[pieces, :, cols].reshape(chunk, HD)
            score = lax.dot_general(
                query, kwin[seen], (((1,), (1,)), ((), ())), preferred_element_type=jnp.float32
            )
            score = score + bias[lower : lower + chunk, :]
            peak = jnp.max(score, axis=-1, keepdims=True)
            weight = jnp.exp2((score - peak) * factor)
            total = jnp.sum(weight, axis=-1, keepdims=True)
            mixed = jnp.dot(
                weight.astype(jnp.bfloat16), vwin[seen], preferred_element_type=jnp.float32
            )
            mixed = mixed * (1.0 / total)
            obuf[h, pieces] = mixed.astype(jnp.bfloat16).reshape(chunk // piece, piece, HD)

        @pl.loop(0, nctx)
        def _(owner):
            sbuf[h, owner] = obuf[h, pick[owner]]

        @pl.loop(1, nctx)
        def _(t):
            o_copy(h, t).start()

        rbuf[h, ctx] = sbuf[h, ctx]

    for h in range(heads):
        arrived = rbuf.at[h, pl.ds(0, nctx - 1)]
        pltpu.make_async_copy(arrived, arrived, o_recv.at[h]).wait()
    for h in range(heads):
        for place in range(count):
            source = slots[ctx * count + place] // count
            o_ref[place * piece : (place + 1) * piece, h * HD : (h + 1) * HD] = rbuf[h, source]

    for h in range(heads):
        left = sbuf.at[h, pl.ds(0, nctx - 1)]
        pltpu.make_async_copy(left, left, o_send.at[h]).wait()

    @pl.loop(1, nhead)
    def _(t):
        q_copy(t).wait_send()

    for which in range(2):
        for step in range(1, reach + 1):
            kv_copy(which, step).wait_send()
        for step in range(reach + 1):
            pass_copy(which, step).wait_send()


def solution(mesh):
    nctx, nhead = mesh.shape["ctx"], mesh.shape["head"]

    def local(queries, keys, values, doc_lengths, slot_source):
        piece, width = queries.shape[0], queries.shape[1] // nhead
        rows = keys.shape[0]
        heads = width // HD
        win = DOC_MAX // rows
        chunk = min(128, rows)
        places = jnp.arange(nhead, dtype=jnp.int32)[None, :]
        mine = slot_source.reshape(nctx, nhead) == lax.axis_index("ctx") * nhead + places
        pick = jnp.sum(jnp.where(mine, places, 0), axis=1)
        dma = pltpu.SemaphoreType.DMA
        return pl.pallas_call(
            functools.partial(kernel, nctx, nhead, win, chunk),
            out_shape=jax.ShapeDtypeStruct((rows, width), jnp.bfloat16),
            in_specs=[pl.BlockSpec(memory_space=pltpu.SMEM)] * 3 + [pl.BlockSpec(memory_space=pl.ANY)] * 3,
            out_specs=pl.BlockSpec(memory_space=pltpu.VMEM),
            scratch_shapes=[
                pltpu.VMEM((rows // piece, piece, width), jnp.bfloat16),
                pltpu.VMEM(((win + 2) * rows, HD), jnp.bfloat16),
                pltpu.VMEM(((win + 2) * rows, HD), jnp.bfloat16),
                pltpu.VMEM((rows, (win + 1) * rows), jnp.float32),
                pltpu.VMEM((heads, rows // piece, piece, HD), jnp.bfloat16),
                pltpu.VMEM((heads, nctx, piece, HD), jnp.bfloat16),
                pltpu.VMEM((heads, nctx, piece, HD), jnp.bfloat16),
                dma((3,)),
                dma((nhead,)),
                dma((nhead,)),
                dma((2, win // 2 + 1)),
                dma((2, win // 2 + 1)),
                dma((2, win // 2 + 1)),
                dma((2, win // 2 + 1)),
                dma((heads,)),
                dma((heads,)),
            ],
            compiler_params=pltpu.CompilerParams(
                collective_id=0, has_side_effects=True, vmem_limit_bytes=56 * 2**20
            ),
        )(pick, slot_source, doc_lengths, queries, keys, values)

    return jax.shard_map(
        local,
        mesh=mesh,
        in_specs=(P(("ctx", "head"), None), P("ctx", None), P("ctx", None), P(), P()),
        out_specs=P("ctx", "head"),
        check_vma=False,
    )
```

time: 400 us -> 58.8 us (0.15); the launches traced: 393 us -> 58.5 us
  waiting for transfers between devices: 233 us -> 0 us
  starting transfers between devices: 101 us -> 0 us
  Pallas kernels: 0 us -> 55.5 us
  matrix products: 28.9 us -> 0 us
  other arithmetic: 18.5 us -> 0.64 us
  local copies, waits for them, and re-layouts: 8.35 us -> 2.42 us
    ppermute x31 -> x0, waiting for transfers between devices: 212 us -> none  [passed_along(): return lax.ppermute(block, axis, route)]
    ppermute x31 -> x0, starting transfers between devices: 75.9 us -> none  [passed_along(): return lax.ppermute(block, axis, route)]
    pallas_call x0 -> x1, Pallas kernels: none -> 55.5 us  [local(): pl.pallas_call(functools.partial(kernel, nctx, nhead, win, chunk), out_sh...]
    dot_general x66 -> x0, matrix products: 28.9 us -> none  [the longest x32 16.9 us: absorb(): jnp.einsum('hck,kd->hcd', weight.astype(jnp.bfloat16), block[1], preferre...]
    all_to_all x2 -> x0, starting transfers between devices: 24.6 us -> none  [the longest x1 15.9 us: route(): lax.all_to_all(outgoing, 'ctx', split_axis=0, concat_axis=0, tiled=True)]
    all_to_all x2 -> x0, waiting for transfers between devices: 21.5 us -> none  [the longest x1 14.7 us: route(): lax.all_to_all(outgoing, 'ctx', split_axis=0, concat_axis=0, tiled=True)]
    reduce_sum x65 -> x1, other arithmetic: 9.62 us -> 0.63 us  [local(): pick = jnp.sum(jnp.where(mine, places, 0), axis=1)]
    and x32 -> x0, other arithmetic: 4.58 us -> none  [update(): (k_doc[None, :] == q_doc[:, None]) & (k_pos[None, :] <= q_pos[:, None])]
  transfers between devices with their start and end apart: 33 -> 0, of which waited for: 33 -> 0; matrix products, arithmetic and copies ran while one was open for 4% -> 0% of each run, Pallas kernels for 0% -> 0%
where the time goes in v1:
time: 58.8 us; the launch traced here: 58.5 us
  Pallas kernels  55.5 us (94%)
  local copies, waits for them, and re-layouts  2.42 us (4%)
  other arithmetic  0.64 us (1%)
    pallas_call x1, Pallas kernels, local(): pl.pallas_call(functools.partial(kernel, nctx, nhead, win, chunk), out_sh...  55.5 us
    unnamed x3, local copies, waits for them, and re-layouts  2.35 us

profile of v1, /device:TPU:1, one launch (start us, length us, event | category | flops | bytes accessed | tf_op | source)
XLA Modules:
  0.0 58.5 jit_solution(16728938690455441338)
XLA Ops:
  0.0 0.0 copy-start
  0.0 0.7 %copy-done = s32[512]{0:T(512)S(1)} copy-done((s32[512]{0:T(512)S(1)}, s32[512]{0:T(512)}, u32[]{:S(2)}) %copy-start) | copy-done | bytes 2072
  0.7 0.1 reshape.8
  0.8 0.6 %select_reduce_fusion.pick = s32[32]{0:T(128)} fusion(s32[32,16]{1,0:T(8,128)S(1)} %reshape.8, s32[16]{0:T(128)S(1)} %iota_add_fusion), kind=kLoop, calls=%fused_computation | loop fusion | flops 1504 | bytes 2240 | tf_op jit(solution)/shard_map/reduce_sum | solution.py:217
  1.4 55.5 %shard_map.55 = bf16[256,512]{1,0:T(8,128)(2,1)} custom-call(s32[32]{0:T(128)} %select_reduce_fusion.pick, s32[512]{0:T(512)} %slots.1, s32[16]{0:T(128)} %lengths.1, bf16[16,8192]{1,0:T(8,128)(2,1)} %q_ref.1, bf16[256,1024]{1,0:T(8,128)(2,1)} %k_ref.1, bf16[256,1024]{1,0:T(8,128)(2,1)} %v_ref.1), custom_call_target="tpu_custom_call" | custom-call | tf_op jit(solution)/shard_map/pallas_call | solution.py:219
  56.9 1.7 %copy.7 = bf16[256,512]{1,0:T(8,128)(2,1)} copy(bf16[256,512]{1,0:T(8,128)(2,1)} %shard_map.55) | data formatting | bytes 524288
  (1 shorter events, 0.0 us)
Async XLA Ops:
  0.0 0.7 %copy-start = (s32[512]{0:T(512)S(1)}, s32[512]{0:T(512)}, u32[]{:S(2)}) copy-start(s32[512]{0:T(512)} %slots.1) | copy-start | bytes 6148

commit v2 on v1

--- a/solution.py
+++ b/solution.py
@@ -18,7 +18,7 @@
 def kernel(
     nctx, nhead, win, chunk,
     pick, slots, lengths, q_ref, k_ref, v_ref, o_ref,
-    qbuf, kwin, vwin, bias, obuf, sbuf, rbuf,
+    qbuf, kvwin, bias, obuf, sbuf, rbuf,
     own_sem, q_send, q_recv, kv_send, kv_recv, f_send, f_recv, o_send, o_recv,
 ):
     ctx = lax.axis_index("ctx")
@@ -27,11 +27,11 @@
     rows = k_ref.shape[0]
     count = rows // piece
     heads = width // HD
-    chips = nctx // 2
-    reach = win // 2
-    core = lax.rem(ctx, 2)
-    chip = ctx // 2
-    sibling = chip * 2 + 1 - core
+    deep = nctx // 4
+    z, xh, core = ctx // 4, lax.rem(ctx // 2, 2), lax.rem(ctx, 2)
+    above = (lax.rem(z + 1, deep) * 4 + xh * 2 + core, head)
+    opposite = (z * 4 + (1 - xh) * 2 + core, head)
+    sibling = (z * 4 + xh * 2 + 1 - core, head)
 
     barrier = pltpu.get_barrier_semaphore()
 
@@ -47,41 +47,46 @@
 
     kv_cols = pl.ds(pl.multiple_of(((head * heads) // GROUP) * HD, HD), HD)
 
-    def block(index):
-        return pl.ds(pl.multiple_of(index * rows, rows), rows)
-
-    def kv_copy(which, step):
-        src = (k_ref, v_ref)[which]
-        dst = (kwin, vwin)[which]
-        return pltpu.make_async_remote_copy(
-            src_ref=src.at[:, kv_cols],
-            dst_ref=dst.at[block((reach - step) * 2 + core)],
-            send_sem=kv_send.at[which, step],
-            recv_sem=kv_recv.at[which, step],
-            device_id=(lax.rem(chip + step, chips) * 2 + core, head),
-            device_id_type=MESH,
-        )
-
-    def pass_copy(which, step):
-        dst = (kwin, vwin)[which]
-        spot = dst.at[block((reach - step) * 2 + core)]
-        return pltpu.make_async_remote_copy(
-            src_ref=spot,
-            dst_ref=spot,
-            send_sem=f_send.at[which, step],
-            recv_sem=f_recv.at[which, step],
-            device_id=(sibling, head),
-            device_id_type=MESH,
-        )
+    def part(which, step):
+        return kvwin.at[which, pl.ds(pl.multiple_of((step * 2 + core) * rows, rows), rows)]
 
     def own_copy(which):
-        src = (k_ref, v_ref)[which]
-        dst = (kwin, vwin)[which]
-        return pltpu.make_async_copy(src.at[:, kv_cols], dst.at[block(reach * 2 + core)], own_sem.at[which])
-
-    for step in range(1, reach + 1):
-        for which in range(2):
-            kv_copy(which, step).start()
+        return pltpu.make_async_copy((k_ref, v_ref)[which].at[:, kv_cols], part(which, 4), own_sem.at[which])
+
+    routes = [
+        (above, None, 2),
+        (above, 2, 0),
+        (opposite, 2, 1 + 2 * xh),
+        (opposite, (1 - xh) * 4, 3 - 2 * xh),
+    ]
+
+    def kv_copy(i, which):
+        to, source, target = routes[i]
+        src = (k_ref, v_ref)[which].at[:, kv_cols] if source is None else part(which, source)
+        return pltpu.make_async_remote_copy(
+            src_ref=src,
+            dst_ref=part(which, target),
+            send_sem=kv_send.at[i, which],
+            recv_sem=kv_recv.at[i, which],
+            device_id=to,
+            device_id_type=MESH,
+        )
+
+    given = [4, 2, 0, 3 - 2 * xh, 1 + 2 * xh]
+
+    def pass_copy(i, which):
+        where = part(which, given[i])
+        return pltpu.make_async_remote_copy(
+            src_ref=where,
+            dst_ref=where,
+            send_sem=f_send.at[i, which],
+            recv_sem=f_recv.at[i, which],
+            device_id=sibling,
+            device_id_type=MESH,
+        )
+
+    for which in range(2):
+        kv_copy(0, which).start()
     for which in range(2):
         own_copy(which).start()
 
@@ -122,20 +127,29 @@
 
     for which in range(2):
         own_copy(which).wait()
-        pass_copy(which, 0).start()
-    for step in range(1, reach + 1):
+        pass_copy(0, which).start()
+    for which in range(2):
+        kv_copy(0, which).wait_recv()
+        kv_copy(1, which).start()
+        kv_copy(2, which).start()
+        pass_copy(1, which).start()
+    for which in range(2):
+        kv_copy(1, which).wait_recv()
+        kv_copy(3, which).start()
+        pass_copy(2, which).start()
+    for i in (2, 3):
         for which in range(2):
-            kv_copy(which, step).wait_recv()
-            pass_copy(which, step).start()
+            kv_copy(i, which).wait_recv()
+            pass_copy(i + 1, which).start()
     q_own.wait()
 
     @pl.loop(1, nhead)
     def _(t):
         q_copy(t).wait_recv()
 
-    for step in range(reach + 1):
+    for i in range(5):
         for which in range(2):
-            pass_copy(which, step).wait_recv()
+            pass_copy(i, which).wait_recv()
 
     seen = pl.ds(pl.multiple_of(core * rows, rows), keys)
     factor = math.log2(math.e) / HD**0.5
@@ -158,14 +172,14 @@
             pieces = pl.ds(lower // piece, chunk // piece)
             query = qbuf[pieces, :, cols].reshape(chunk, HD)
             score = lax.dot_general(
-                query, kwin[seen], (((1,), (1,)), ((), ())), preferred_element_type=jnp.float32
+                query, kvwin[0, seen], (((1,), (1,)), ((), ())), preferred_element_type=jnp.float32
             )
             score = score + bias[lower : lower + chunk, :]
             peak = jnp.max(score, axis=-1, keepdims=True)
             weight = jnp.exp2((score - peak) * factor)
             total = jnp.sum(weight, axis=-1, keepdims=True)
             mixed = jnp.dot(
-                weight.astype(jnp.bfloat16), vwin[seen], preferred_element_type=jnp.float32
+                weight.astype(jnp.bfloat16), kvwin[1, seen], preferred_element_type=jnp.float32
             )
             mixed = mixed * (1.0 / total)
             obuf[h, pieces] = mixed.astype(jnp.bfloat16).reshape(chunk // piece, piece, HD)
@@ -180,27 +194,28 @@
 
         rbuf[h, ctx] = sbuf[h, ctx]
 
-    for h in range(heads):
-        arrived = rbuf.at[h, pl.ds(0, nctx - 1)]
-        pltpu.make_async_copy(arrived, arrived, o_recv.at[h]).wait()
+    def o_waits(buffer, sem):
+        for h in range(heads):
+            moved = buffer.at[h, pl.ds(0, nctx - 1)]
+            pltpu.make_async_copy(moved, moved, sem.at[h]).wait()
+
+    o_waits(rbuf, o_recv)
     for h in range(heads):
         for place in range(count):
             source = slots[ctx * count + place] // count
             o_ref[place * piece : (place + 1) * piece, h * HD : (h + 1) * HD] = rbuf[h, source]
 
-    for h in range(heads):
-        left = sbuf.at[h, pl.ds(0, nctx - 1)]
-        pltpu.make_async_copy(left, left, o_send.at[h]).wait()
+    o_waits(sbuf, o_send)
 
     @pl.loop(1, nhead)
     def _(t):
         q_copy(t).wait_send()
 
     for which in range(2):
-        for step in range(1, reach + 1):
-            kv_copy(which, step).wait_send()
-        for step in range(reach + 1):
-            pass_copy(which, step).wait_send()
+        for i in range(4):
+            kv_copy(i, which).wait_send()
+        for i in range(5):
+            pass_copy(i, which).wait_send()
 
 
 def solution(mesh):
@@ -223,8 +238,7 @@
             out_specs=pl.BlockSpec(memory_space=pltpu.VMEM),
             scratch_shapes=[
                 pltpu.VMEM((rows // piece, piece, width), jnp.bfloat16),
-                pltpu.VMEM(((win + 2) * rows, HD), jnp.bfloat16),
-                pltpu.VMEM(((win + 2) * rows, HD), jnp.bfloat16),
+                pltpu.VMEM((2, (win + 2) * rows, HD), jnp.bfloat16),
                 pltpu.VMEM((rows, (win + 1) * rows), jnp.float32),
                 pltpu.VMEM((heads, rows // piece, piece, HD), jnp.bfloat16),
                 pltpu.VMEM((heads, nctx, piece, HD), jnp.bfloat16),
@@ -232,10 +246,10 @@
                 dma((3,)),
                 dma((nhead,)),
                 dma((nhead,)),
-                dma((2, win // 2 + 1)),
-                dma((2, win // 2 + 1)),
-                dma((2, win // 2 + 1)),
-                dma((2, win // 2 + 1)),
+                dma((4, 2)),
+                dma((4, 2)),
+                dma((5, 2)),
+                dma((5, 2)),
                 dma((heads,)),
                 dma((heads,)),
             ],

time: 58.8 us -> 52.5 us (0.89)
  Pallas kernels: 55.5 us -> 49.1 us
    pallas_call x1, Pallas kernels: 55.5 us -> 49.1 us  [local(): pl.pallas_call(functools.partial(kernel, nctx, nhead, win, chunk), out_sh...]
where the time goes in v2:
time: 52.5 us; the launch traced here: 52.2 us
  Pallas kernels  49.1 us (94%)
  local copies, waits for them, and re-layouts  2.42 us (5%)
  other arithmetic  0.64 us (1%)
    pallas_call x1, Pallas kernels, local(): pl.pallas_call(functools.partial(kernel, nctx, nhead, win, chunk), out_sh...  49.1 us
    unnamed x3, local copies, waits for them, and re-layouts  2.35 us

profile of v2, /device:TPU:1, one launch (start us, length us, event | category | flops | bytes accessed | tf_op | source)
XLA Modules:
  0.0 52.2 jit_solution(13661755944471500461)
XLA Ops:
  0.0 0.0 copy-start
  0.0 0.7 %copy-done = s32[512]{0:T(512)S(1)} copy-done((s32[512]{0:T(512)S(1)}, s32[512]{0:T(512)}, u32[]{:S(2)}) %copy-start) | copy-done | bytes 2072
  0.7 0.1 reshape.8
  0.8 0.6 %select_reduce_fusion.pick = s32[32]{0:T(128)} fusion(s32[32,16]{1,0:T(8,128)S(1)} %reshape.8, s32[16]{0:T(128)S(1)} %iota_add_fusion), kind=kLoop, calls=%fused_computation | loop fusion | flops 1504 | bytes 2240 | tf_op jit(solution)/shard_map/reduce_sum | solution.py:232
  1.4 49.1 %shard_map.55 = bf16[256,512]{1,0:T(8,128)(2,1)} custom-call(s32[32]{0:T(128)} %select_reduce_fusion.pick, s32[512]{0:T(512)} %slots.1, s32[16]{0:T(128)} %lengths.1, bf16[16,8192]{1,0:T(8,128)(2,1)} %q_ref.1, bf16[256,1024]{1,0:T(8,128)(2,1)} %k_ref.1, bf16[256,1024]{1,0:T(8,128)(2,1)} %v_ref.1), custom_call_target="tpu_custom_call" | custom-call | tf_op jit(solution)/shard_map/pallas_call | solution.py:234
  50.5 1.7 %copy.7 = bf16[256,512]{1,0:T(8,128)(2,1)} copy(bf16[256,512]{1,0:T(8,128)(2,1)} %shard_map.55) | data formatting | bytes 524288
  (1 shorter events, 0.0 us)
Async XLA Ops:
  0.0 0.7 %copy-start = (s32[512]{0:T(512)S(1)}, s32[512]{0:T(512)}, u32[]{:S(2)}) copy-start(s32[512]{0:T(512)} %slots.1) | copy-start | bytes 6148

commit v3 on v2

--- a/solution.py
+++ b/solution.py
@@ -12,13 +12,19 @@
 GROUP = 8
 DOC_MAX = 2048
 MASKED = -1e30
+CUTS = 2
 MESH = pl.DeviceIdType.MESH
+
+
+def turn(t, n):
+    side = (n - t + 1) // 2
+    return jnp.where((n - t) % 2 == 1, side, n - side)
 
 
 def kernel(
     nctx, nhead, win, chunk,
-    pick, slots, lengths, q_ref, k_ref, v_ref, o_ref,
-    qbuf, kvwin, bias, obuf, sbuf, rbuf,
+    slots, table, lengths, q_ref, k_ref, v_ref, o_ref,
+    qbuf, kvwin, bias, obuf, sbuf, rbuf, chosen, pick,
     own_sem, q_send, q_recv, kv_send, kv_recv, f_send, f_recv, o_send, o_recv,
 ):
     ctx = lax.axis_index("ctx")
@@ -47,11 +53,17 @@
 
     kv_cols = pl.ds(pl.multiple_of(((head * heads) // GROUP) * HD, HD), HD)
 
-    def part(which, step):
-        return kvwin.at[which, pl.ds(pl.multiple_of((step * 2 + core) * rows, rows), rows)]
-
-    def own_copy(which):
-        return pltpu.make_async_copy((k_ref, v_ref)[which].at[:, kv_cols], part(which, 4), own_sem.at[which])
+    cut = rows // CUTS
+    parts = range(2 * CUTS)
+
+    def part(n, step):
+        return kvwin.at[n // CUTS, pl.ds(pl.multiple_of((step * 2 + core) * rows + n % CUTS * cut, cut), cut)]
+
+    def block(n):
+        return (k_ref, v_ref)[n // CUTS].at[pl.ds(n % CUTS * cut, cut), kv_cols]
+
+    def own_copy(n):
+        return pltpu.make_async_copy(block(n), part(n, 4), own_sem.at[n])
 
     routes = [
         (above, None, 2),
@@ -60,35 +72,35 @@
         (opposite, (1 - xh) * 4, 3 - 2 * xh),
     ]
 
-    def kv_copy(i, which):
+    def kv_copy(i, n):
         to, source, target = routes[i]
-        src = (k_ref, v_ref)[which].at[:, kv_cols] if source is None else part(which, source)
+        src = block(n) if source is None else part(n, source)
         return pltpu.make_async_remote_copy(
             src_ref=src,
-            dst_ref=part(which, target),
-            send_sem=kv_send.at[i, which],
-            recv_sem=kv_recv.at[i, which],
+            dst_ref=part(n, target),
+            send_sem=kv_send.at[i, n],
+            recv_sem=kv_recv.at[i, n],
             device_id=to,
             device_id_type=MESH,
         )
 
     given = [4, 2, 0, 3 - 2 * xh, 1 + 2 * xh]
 
-    def pass_copy(i, which):
-        where = part(which, given[i])
+    def pass_copy(i, n):
+        where = part(n, given[i])
         return pltpu.make_async_remote_copy(
             src_ref=where,
             dst_ref=where,
-            send_sem=f_send.at[i, which],
-            recv_sem=f_recv.at[i, which],
+            send_sem=f_send.at[i, n],
+            recv_sem=f_recv.at[i, n],
             device_id=sibling,
             device_id_type=MESH,
         )
 
-    for which in range(2):
-        kv_copy(0, which).start()
-    for which in range(2):
-        own_copy(which).start()
+    for n in parts:
+        kv_copy(0, n).start()
+    for n in parts:
+        own_copy(n).start()
 
     def q_copy(t):
         peer = lax.rem(head + t, nhead)
@@ -106,9 +118,20 @@
         q_copy(t).start()
 
     q_own = pltpu.make_async_copy(
-        q_ref.at[:, pl.ds(pl.multiple_of(head * width, width), width)], qbuf.at[head], own_sem.at[2]
+        q_ref.at[:, pl.ds(pl.multiple_of(head * width, width), width)], qbuf.at[head], own_sem.at[2 * CUTS]
     )
     q_own.start()
+
+    lanes = lax.broadcasted_iota(jnp.int32, table.shape, 1) % count
+    found = jnp.where(table[...] == ctx * count + lanes, lanes, 0)
+    shift = count // 2
+    while shift:
+        found = found + pltpu.roll(found, table.shape[1] - shift, 1)
+        shift //= 2
+    chosen[...] = found
+    pick_copy = pltpu.make_async_copy(chosen, pick, own_sem.at[2 * CUTS + 1])
+    pick_copy.start()
+    across = table.shape[1] // count
 
     keys = (win + 1) * rows
     for lower in range(0, rows, chunk):
@@ -125,22 +148,22 @@
             allowed = (at >= start) & (at <= win * rows + line)
             bias[lower : lower + chunk, col : col + rows] = jnp.where(allowed, 0.0, MASKED)
 
-    for which in range(2):
-        own_copy(which).wait()
-        pass_copy(0, which).start()
-    for which in range(2):
-        kv_copy(0, which).wait_recv()
-        kv_copy(1, which).start()
-        kv_copy(2, which).start()
-        pass_copy(1, which).start()
-    for which in range(2):
-        kv_copy(1, which).wait_recv()
-        kv_copy(3, which).start()
-        pass_copy(2, which).start()
+    for n in parts:
+        own_copy(n).wait()
+        pass_copy(0, n).start()
+    for n in parts:
+        kv_copy(0, n).wait_recv()
+        kv_copy(1, n).start()
+        kv_copy(2, n).start()
+        pass_copy(1, n).start()
+    for n in parts:
+        kv_copy(1, n).wait_recv()
+        kv_copy(3, n).start()
+        pass_copy(2, n).start()
     for i in (2, 3):
-        for which in range(2):
-            kv_copy(i, which).wait_recv()
-            pass_copy(i + 1, which).start()
+        for n in parts:
+            kv_copy(i, n).wait_recv()
+            pass_copy(i + 1, n).start()
     q_own.wait()
 
     @pl.loop(1, nhead)
@@ -148,9 +171,10 @@
         q_copy(t).wait_recv()
 
     for i in range(5):
-        for which in range(2):
-            pass_copy(i, which).wait_recv()
-
+        for n in parts:
+            pass_copy(i, n).wait_recv()
+
+    pick_copy.wait()
     seen = pl.ds(pl.multiple_of(core * rows, rows), keys)
     factor = math.log2(math.e) / HD**0.5
 
@@ -186,11 +210,11 @@
 
         @pl.loop(0, nctx)
         def _(owner):
-            sbuf[h, owner] = obuf[h, pick[owner]]
+            sbuf[h, owner] = obuf[h, pick[owner // across, owner % across * count]]
 
         @pl.loop(1, nctx)
         def _(t):
-            o_copy(h, t).start()
+            o_copy(h, turn(t, nctx)).start()
 
         rbuf[h, ctx] = sbuf[h, ctx]
 
@@ -211,11 +235,11 @@
     def _(t):
         q_copy(t).wait_send()
 
-    for which in range(2):
+    for n in parts:
         for i in range(4):
-            kv_copy(i, which).wait_send()
+            kv_copy(i, n).wait_send()
         for i in range(5):
-            pass_copy(i, which).wait_send()
+            pass_copy(i, n).wait_send()
 
 
 def solution(mesh):
@@ -227,14 +251,17 @@
         heads = width // HD
         win = DOC_MAX // rows
         chunk = min(128, rows)
-        places = jnp.arange(nhead, dtype=jnp.int32)[None, :]
-        mine = slot_source.reshape(nctx, nhead) == lax.axis_index("ctx") * nhead + places
-        pick = jnp.sum(jnp.where(mine, places, 0), axis=1)
+        table = slot_source.reshape(-1, min(128, slot_source.shape[0]))
         dma = pltpu.SemaphoreType.DMA
         return pl.pallas_call(
             functools.partial(kernel, nctx, nhead, win, chunk),
             out_shape=jax.ShapeDtypeStruct((rows, width), jnp.bfloat16),
-            in_specs=[pl.BlockSpec(memory_space=pltpu.SMEM)] * 3 + [pl.BlockSpec(memory_space=pl.ANY)] * 3,
+            in_specs=[
+                pl.BlockSpec(memory_space=pltpu.SMEM),
+                pl.BlockSpec(memory_space=pltpu.VMEM),
+                pl.BlockSpec(memory_space=pltpu.SMEM),
+            ]
+            + [pl.BlockSpec(memory_space=pl.ANY)] * 3,
             out_specs=pl.BlockSpec(memory_space=pltpu.VMEM),
             scratch_shapes=[
                 pltpu.VMEM((rows // piece, piece, width), jnp.bfloat16),
@@ -243,20 +270,22 @@
                 pltpu.VMEM((heads, rows // piece, piece, HD), jnp.bfloat16),
                 pltpu.VMEM((heads, nctx, piece, HD), jnp.bfloat16),
                 pltpu.VMEM((heads, nctx, piece, HD), jnp.bfloat16),
-                dma((3,)),
+                pltpu.VMEM(table.shape, jnp.int32),
+                pltpu.SMEM(table.shape, jnp.int32),
+                dma((2 * CUTS + 2,)),
                 dma((nhead,)),
                 dma((nhead,)),
-                dma((4, 2)),
-                dma((4, 2)),
-                dma((5, 2)),
-                dma((5, 2)),
+                dma((4, 2 * CUTS)),
+                dma((4, 2 * CUTS)),
+                dma((5, 2 * CUTS)),
+                dma((5, 2 * CUTS)),
                 dma((heads,)),
                 dma((heads,)),
             ],
             compiler_params=pltpu.CompilerParams(
                 collective_id=0, has_side_effects=True, vmem_limit_bytes=56 * 2**20
             ),
-        )(pick, slot_source, doc_lengths, queries, keys, values)
+        )(slot_source, table, doc_lengths, queries, keys, values)
 
     return jax.shard_map(
         local,

time: 52.5 us -> 50.3 us (0.958)
  local copies, waits for them, and re-layouts: 2.42 us -> 1.67 us
  Pallas kernels: 49.1 us -> 48.4 us
  other arithmetic: 0.64 us -> 0 us
    pallas_call x1, Pallas kernels: 49.1 us -> 48.4 us  [local(): pl.pallas_call(functools.partial(kernel, nctx, nhead, win, chunk), out_sh...]
    unnamed x3 -> x1, local copies, waits for them, and re-layouts: 2.35 us -> 1.67 us
    reduce_sum x1 -> x0, other arithmetic: 0.63 us -> none  [local(): pick = jnp.sum(jnp.where(mine, places, 0), axis=1)]
where the time goes in v3:
time: 50.3 us; the launch traced here: 50.1 us
  Pallas kernels  48.4 us (96%)
  local copies, waits for them, and re-layouts  1.67 us (3%)
    pallas_call x1, Pallas kernels, local(): pl.pallas_call(functools.partial(kernel, nctx, nhead, win, chunk), out_sh...  48.4 us
    unnamed x1, local copies, waits for them, and re-layouts  1.67 us

profile of v3, /device:TPU:1, one launch (start us, length us, event | category | flops | bytes accessed | tf_op | source)
XLA Modules:
  0.0 50.1 jit_solution(2963675390334725202)
XLA Ops:
  0.0 48.4 %shard_map.55 = bf16[256,512]{1,0:T(8,128)(2,1)} custom-call(s32[512]{0:T(512)} %slots.1, s32[4,128]{1,0:T(4,128)} %bitcast.1, s32[16]{0:T(128)} %lengths.1, bf16[16,8192]{1,0:T(8,128)(2,1)} %q_ref.1, bf16[256,1024]{1,0:T(8,128)(2,1)} %k_ref.1, bf16[256,1024]{1,0:T(8,128)(2,1)} %v_ref.1), custom_call_target="tpu_custom_call" | custom-call | tf_op jit(solution)/shard_map/pallas_call | solution.py:256
  48.4 1.7 %copy.7 = bf16[256,512]{1,0:T(8,128)(2,1)} copy(bf16[256,512]{1,0:T(8,128)(2,1)} %shard_map.55) | data formatting | bytes 524288

commit v4 on v3

--- a/solution.py
+++ b/solution.py
@@ -25,7 +25,7 @@
     nctx, nhead, win, chunk,
     slots, table, lengths, q_ref, k_ref, v_ref, o_ref,
     qbuf, kvwin, bias, obuf, sbuf, rbuf, chosen, pick,
-    own_sem, q_send, q_recv, kv_send, kv_recv, f_send, f_recv, o_send, o_recv,
+    own_sem, q_send, q_recv, kv_send, kv_recv, f_send, f_recv, o_send, o_recv, token,
 ):
     ctx = lax.axis_index("ctx")
     head = lax.axis_index("head")
@@ -35,21 +35,25 @@
     heads = width // HD
     deep = nctx // 4
     z, xh, core = ctx // 4, lax.rem(ctx // 2, 2), lax.rem(ctx, 2)
-    above = (lax.rem(z + 1, deep) * 4 + xh * 2 + core, head)
+
+    def along(distance):
+        return (lax.rem(z + distance + deep, deep) * 4 + xh * 2 + core, head)
+
+    above = along(1)
     opposite = (z * 4 + (1 - xh) * 2 + core, head)
     sibling = (z * 4 + xh * 2 + 1 - core, head)
 
     barrier = pltpu.get_barrier_semaphore()
-
-    @pl.loop(1, nctx)
-    def _(t):
-        pl.semaphore_signal(barrier, device_id=(lax.rem(ctx + t, nctx), head), device_id_type=MESH)
+    near = [along(1), along(-1), along(2), along(-2), opposite, sibling]
+    near.append((z * 4 + (1 - xh) * 2 + 1 - core, head))
+    for peer in near:
+        pl.semaphore_signal(barrier, device_id=peer, device_id_type=MESH)
 
     @pl.loop(1, nhead)
     def _(t):
         pl.semaphore_signal(barrier, device_id=(ctx, lax.rem(head + t, nhead)), device_id_type=MESH)
 
-    pl.semaphore_wait(barrier, nctx + nhead - 2)
+    pl.semaphore_wait(barrier, nhead - 1 + len(near))
 
     kv_cols = pl.ds(pl.multiple_of(((head * heads) // GROUP) * HD, HD), HD)
 
@@ -121,6 +125,9 @@
         q_ref.at[:, pl.ds(pl.multiple_of(head * width, width), width)], qbuf.at[head], own_sem.at[2 * CUTS]
     )
     q_own.start()
+
+    for i, distance in enumerate((1, -1, 2, -2)):
+        pl.semaphore_signal(token.at[i], device_id=along(distance), device_id_type=MESH)
 
     lanes = lax.broadcasted_iota(jnp.int32, table.shape, 1) % count
     found = jnp.where(table[...] == ctx * count + lanes, lanes, 0)
@@ -156,6 +163,10 @@
         kv_copy(1, n).start()
         kv_copy(2, n).start()
         pass_copy(1, n).start()
+    for i in range(4):
+        pl.semaphore_wait(token.at[i], 1)
+    for i, distance in enumerate((2, -2)):
+        pl.semaphore_signal(token.at[4 + i], device_id=along(distance), device_id_type=MESH)
     for n in parts:
         kv_copy(1, n).wait_recv()
         kv_copy(3, n).start()
@@ -174,6 +185,8 @@
         for n in parts:
             pass_copy(i, n).wait_recv()
 
+    for i in range(2):
+        pl.semaphore_wait(token.at[4 + i], 1)
     pick_copy.wait()
     seen = pl.ds(pl.multiple_of(core * rows, rows), keys)
     factor = math.log2(math.e) / HD**0.5
@@ -281,6 +294,7 @@
                 dma((5, 2 * CUTS)),
                 dma((heads,)),
                 dma((heads,)),
+                pltpu.SemaphoreType.REGULAR((6,)),
             ],
             compiler_params=pltpu.CompilerParams(
                 collective_id=0, has_side_effects=True, vmem_limit_bytes=56 * 2**20

time: 50.3 us -> 49.8 us (0.990)
  no operation moved by 1% of the time
where the time goes in v4:
time: 49.8 us; the launch traced here: 49.6 us
  Pallas kernels  47.9 us (96%)
  local copies, waits for them, and re-layouts  1.67 us (3%)
    pallas_call x1, Pallas kernels, local(): pl.pallas_call(functools.partial(kernel, nctx, nhead, win, chunk), out_sh...  47.9 us
    unnamed x1, local copies, waits for them, and re-layouts  1.67 us

profile of v4, /device:TPU:1, one launch (start us, length us, event | category | flops | bytes accessed | tf_op | source)
XLA Modules:
  0.0 49.6 jit_solution(10218446439373622368)
XLA Ops:
  0.0 47.9 %shard_map.55 = bf16[256,512]{1,0:T(8,128)(2,1)} custom-call(s32[512]{0:T(512)} %slots.1, s32[4,128]{1,0:T(4,128)} %bitcast.1, s32[16]{0:T(128)} %lengths.1, bf16[16,8192]{1,0:T(8,128)(2,1)} %q_ref.1, bf16[256,1024]{1,0:T(8,128)(2,1)} %k_ref.1, bf16[256,1024]{1,0:T(8,128)(2,1)} %v_ref.1), custom_call_target="tpu_custom_call" | custom-call | tf_op jit(solution)/shard_map/pallas_call | solution.py:269
  47.9 1.7 %copy.7 = bf16[256,512]{1,0:T(8,128)(2,1)} copy(bf16[256,512]{1,0:T(8,128)(2,1)} %shard_map.55) | data formatting | bytes 524288
